TPU v7x, 32 devices: a whole 2x2x4 slice. The times are simulated.
32 devices in a mesh: seq: 4 (over y, x), dp: 4 (over z), enc: 2 (over core).
Axes of the slice: x: 2, y: 2, z: 4, core: 2. Of those that a mesh axis runs over, the one named last changes fastest.
Arguments:
- lm_grad: bfloat16 [4, 4, 192, 1152], P('dp', 'enc', 'seq'), may hold values from -6 to 6
- image_tokens: int32 [4, 4, 4], P('dp'), may hold values from 1 to 15, as said below
- image_offset: int32 [4, 4, 4], P('dp'), may hold values from 0 to 47, as said below
- image_owner: int32 [4, 4, 4], P('dp'), may hold values from 0 to 3, as said below
- mlp_input: bfloat16 [4, 4, 240, 1152], P('dp', None, 'seq'), may hold values from -36 to 36
- layer_output: bfloat16 [4, 4, 240, 1152], P('dp', 'enc', 'seq'), may hold values from -36 to 36
- pre_gain: float32 [1152], replicated, may hold values from 0.5 to 1.5
- pre_bias: float32 [1152], replicated, may hold values from -3 to 3
- fc1_weight: bfloat16 [1152, 4304], P(None, 'enc'), may hold values from -0.1875 to 0.1875
- fc1_bias: float32 [4304], P('enc'), may hold values from -3 to 3
- fc2_weight: bfloat16 [4304, 1152], P('enc'), may hold values from -0.09375 to 0.09375
- post_gain: float32 [1152], replicated, may hold values from 0.5 to 1.5
- post_bias: float32 [1152], replicated, may hold values from -3 to 3
- merge_gain: float32 [1152], replicated, may hold values from 0.5 to 1.5
Outputs:
- act_grad: bfloat16 [4, 4, 240, 1152], P('dp', 'enc', 'seq')
- norm_grads: float32 [6, 1152], replicated
- fc1_bias_grad: float32 [4304], replicated
Inputs may be any that keep to these rules, and one draw needn't show every extreme that they name: `image_tokens`: the 4 images of one LM shard have token counts that sum to 48, and one of them has 15. `image_offset`: the images of one LM shard lie back to back over its 48 rows, in some order; each entry is an image's first row in its shard. Images are placed round-robin by their index j in a shard: image_owner[r, q, j] = (q + image_owner[r, 0, j]) mod 4, with the 4 values image_owner[r, 0, j] different. So each encoder chip owns exactly 4 images of its replica, the visual tokens owned by one chip number at most 60, and some chip owns exactly 60.
All inputs are finite; a program needn't handle non-finite values.
Results may differ from a plain program's by a relative error of at most 0.005.
Values may be sent and summed in bfloat16 or wider, within the bound.
A program may use at most 64 MiB of HBM per device.

v0:
```python
import math
import jax
import jax.numpy as jnp
from jax import lax
from jax.sharding import PartitionSpec as P

D = 1152
FF = 4304
PATCH_GROUP = 4
ROWS_DEV = 48
CAP_TOK = 60
EPSILON = 1e-06
SLOPE_K = math.sqrt(2.0 / math.pi)
CUBIC = 0.044715


def layer_norm(values):
    row_mean = jnp.mean(values, axis=-1, keepdims=True)
    centred = values - row_mean
    return centred * lax.rsqrt(jnp.mean(centred * centred, axis=-1, keepdims=True) + EPSILON)


def rms_norm(values):
    return values * lax.rsqrt(jnp.mean(values * values, axis=-1, keepdims=True) + EPSILON)


def gelu_slope(pre_act):
    inner_arg = SLOPE_K * (pre_act + CUBIC * pre_act * pre_act * pre_act)
    tangent = jnp.tanh(inner_arg)
    return 0.5 * (1.0 + tangent) + 0.5 * pre_act * (1.0 - tangent * tangent) * SLOPE_K * (
        1.0 + 3.0 * CUBIC * pre_act * pre_act
    )


def head_back(incoming, layer_rows, merge_gain, post_gain, post_bias):

    def merge_head(row_values, merge_scale, post_scale, post_shift):
        return rms_norm(layer_norm(row_values) * post_scale + post_shift) * merge_scale

    _, pullback = jax.vjp(
        merge_head, layer_rows.astype(jnp.float32), merge_gain, post_gain, post_bias
    )
    return pullback(incoming.astype(jnp.float32))


def pre_back(input_rows, pre_gain, pre_bias, upstream):

    def prenorm(row_values, scale_vec, shift_vec):
        return layer_norm(row_values) * scale_vec + shift_vec

    _, pullback = jax.vjp(prenorm, input_rows.astype(jnp.float32), pre_gain, pre_bias)
    return pullback(upstream)


def slot_source(lengths, offsets, owners, chip_index):
    shard_count = lengths.shape[0]
    is_mine = owners == chip_index
    my_len = jnp.sum(jnp.where(is_mine, lengths, 0), axis=1)
    my_off = jnp.sum(jnp.where(is_mine, offsets, 0), axis=1)
    slot_first = jnp.cumsum(my_len) - my_len
    slot_ids = jnp.arange(CAP_TOK, dtype=jnp.int32)
    inside = (slot_ids[:, None] >= slot_first[None, :]) & (
        slot_ids[:, None] < (slot_first + my_len)[None, :]
    )
    live_slot = jnp.any(inside, axis=1)
    shard_ids = jnp.arange(shard_count, dtype=jnp.int32)
    source = jnp.sum(jnp.where(inside, shard_ids[None, :], 0), axis=1)
    token_index = slot_ids - jnp.sum(jnp.where(inside, slot_first[None, :], 0), axis=1)
    shard_row = jnp.sum(jnp.where(inside, my_off[None, :], 0), axis=1) + token_index
    return (live_slot, source, token_index, shard_row)


def body(
    lm_grad,
    image_tokens,
    image_offset,
    image_owner,
    mlp_input,
    layer_output,
    pre_gain,
    pre_bias,
    fc1_weight,
    fc1_bias,
    fc2_weight,
    post_gain,
    post_bias,
    merge_gain,
):
    chip_index = lax.axis_index("seq")
    core_index = lax.axis_index("enc")
    shards = lax.axis_size("seq")
    own_patches = PATCH_GROUP // lax.axis_size("enc")
    lengths = image_tokens[0]
    offsets = image_offset[0]
    owners = image_owner[0]
    live_slot, source, token_index, shard_row = slot_source(lengths, offsets, owners, chip_index)
    own_rows = lm_grad[0]
    global_row = source * ROWS_DEV + shard_row
    portion = lax.all_gather(own_rows, "seq", axis=1, tiled=True)
    row_count = portion.shape[1]
    inside_piece = live_slot & (global_row >= 0) & (global_row < row_count)
    taken = jnp.take(portion, jnp.clip(global_row, 0, row_count - 1), axis=1)
    incoming = jnp.where(inside_piece[None, :, None], taken, jnp.zeros_like(taken))
    res_grad, merge_grad, post_grad, shift_grad = head_back(
        incoming, layer_output[0], merge_gain, post_gain, post_bias
    )
    res_wire = res_grad.astype(jnp.bfloat16)
    all_res = lax.all_gather(res_wire, "enc", axis=0, tiled=True)
    input_rows = mlp_input[0]
    normed = (layer_norm(input_rows.astype(jnp.float32)) * pre_gain + pre_bias).astype(jnp.bfloat16)
    pre_act = (
        jnp.dot(normed.reshape(-1, D), fc1_weight, preferred_element_type=jnp.float32) + fc1_bias
    )
    down_back = lax.dot_general(
        all_res.reshape(-1, D),
        fc2_weight,
        (((1,), (1,)), ((), ())),
        preferred_element_type=jnp.float32,
    )
    hidden_grad = down_back * gelu_slope(pre_act)
    fc1_part = jnp.sum(hidden_grad, axis=0)
    hidden_units = fc1_bias.shape[0]
    hidden_wire = hidden_grad.astype(jnp.bfloat16).reshape(PATCH_GROUP, CAP_TOK, hidden_units)
    portion = hidden_wire
    product = lax.dot_general(
        portion.reshape(-1, hidden_units),
        fc1_weight,
        (((1,), (1,)), ((), ())),
        preferred_element_type=jnp.float32,
    )
    summed = lax.psum(product.reshape(PATCH_GROUP, CAP_TOK, D), "enc")
    upstream = lax.dynamic_slice_in_dim(summed, core_index * own_patches, own_patches, 0)
    own_input = lax.dynamic_slice_in_dim(input_rows, core_index * own_patches, own_patches, 0)
    input_grad, pre_scale_grad, pre_shift_grad = pre_back(own_input, pre_gain, pre_bias, upstream)
    act_grad = (res_grad + input_grad).astype(jnp.bfloat16)[None]
    fc2_part = jnp.sum(res_grad, axis=(0, 1))
    norm_part = jnp.stack(
        [merge_grad, post_grad, shift_grad, fc2_part, pre_scale_grad, pre_shift_grad]
    )
    fc1_full = lax.dynamic_update_slice_in_dim(
        jnp.zeros((FF,), jnp.float32), fc1_part, core_index * hidden_units, 0
    )
    norm_sum, fc1_sum = lax.psum((norm_part, fc1_full), ("seq", "dp", "enc"))
    grad_scale = 1.0 / math.sqrt(PATCH_GROUP * ROWS_DEV * shards * lax.axis_size("dp"))
    return (act_grad, norm_sum * grad_scale, fc1_sum * grad_scale)


def solution(mesh):
    in_specs = (
        P("dp", "enc", "seq", None),
        P("dp", None, None),
        P("dp", None, None),
        P("dp", None, None),
        P("dp", None, "seq", None),
        P("dp", "enc", "seq", None),
        P(),
        P(),
        P(None, "enc"),
        P("enc"),
        P("enc", None),
        P(),
        P(),
        P(),
    )
    out_specs = (P("dp", "enc", "seq", None), P(), P())
    return jax.shard_map(body, mesh=mesh, in_specs=in_specs, out_specs=out_specs, check_vma=False)
```

profile of v0, /device:TPU:0, one launch (start us, length us, event | category | flops | bytes accessed | tf_op | source)
XLA Modules:
  0.0 126.4 jit_solution(4036860565229651967)
XLA Ops:
  7.2 0.0 copy-start.2
  7.2 0.0 all-reduce.3.cloned.1.call-start
  7.2 0.9 select_reduce_fusion.2
  8.1 0.2 reduce-window.7
  8.3 0.1 fusion.43
  8.4 0.1 select_reduce_fusion.3
  8.5 1.3 %convert_reduce_fusion.2 = f32[4,60]{0,1:T(8,128)S(1)} fusion(bf16[1,4,60,1152]{3,1,2,0:T(4,128)(2,1)} %param.18), kind=kLoop, calls=%fused_computation.44 | loop fusion | flops 552720 | bytes 553920 | tf_op jit(solution)/shard_map/reduce_sum | solution.py:18
  9.9 1.6 %fusion.6 = f32[4,60]{0,1:T(8,128)S(1)} fusion(bf16[1,4,60,1152]{3,1,2,0:T(4,128)(2,1)} %param.18, f32[4,60]{0,1:T(8,128)S(1)} %broadcast_multiply_fusion.2), kind=kLoop, calls=%fused_computation.12 | loop fusion | flops 1105680 | bytes 554880 | tf_op jit(solution)/shard_map/reduce_sum | solution.py:20
  11.5 0.1 copy.81
  11.6 1.1 copy.66
  12.7 0.0 copy-start.5
  12.7 0.2 copy.52
  12.9 13.7 %all-gather = bf16[1,2,192,1152]{3,1,0,2:T(2,128)(2,1)S(1)} all-gather(bf16[1,2,48,1152]{3,1,0,2:T(2,128)(2,1)S(1)} %copy.52), channel_id=2, replica_groups=mesh['seq'=4,'dp'=4,'enc'=2] {'seq'}, dimensions={2}, use_global_device_ids=true | all-gather | bytes 1105920 | tf_op jit(solution)/shard_map/all_gather | solution.py:99
  26.6 0.3 convert_reduce_fusion.1
  26.9 0.5 fusion.14
  27.4 0.1 copy.55
  27.5 0.1 copy.56
  27.6 0.0 copy-done.3
  27.6 0.0 copy-done.4
  27.6 0.7 multiply_reduce_fusion.1
  28.3 0.1 copy.57
  28.4 0.1 copy.58
  28.6 1.2 gather_fusion
  29.7 1.7 %fusion.27 = (f32[1152]{0:T(1024)S(1)}, f32[2,60]{0,1:T(8,128)S(1)}, bf16[60,2,1152]{2,1,0:T(2,128)(2,1)S(1)}) fusion(f32[2,60]{0,1:T(8,128)S(1)} %copy.58, f32[1152]{0:T(1024)S(1)} %copy-done.4, f32[1152]{0:T(1024)S(1)} %copy-done.3, f32[2,60]{0,1:T(8,128)S(1)} %copy.56, f32[2,60]{0,1:T(8,128)S(1)} %broadcast_multiply_fusion.3, ...), kind=kLoop, calls=%fused_computation.43 | loop fusion | flops 1934088 | bytes 849912 | tf_op jit(solution)/shard_map/transpose(jvp())/reduce_sum | solution.py:38
  31.5 0.1 copy.59
  31.6 0.1 copy.60
  31.7 1.9 %multiply_reduce_fusion = (f32[1152]{0:T(1024)S(1)}, f32[2,60]{0,1:T(8,128)S(1)}, f32[1152]{0:T(1024)S(1)}, f32[2,60,1152]{2,0,1:T(2,128)S(1)}) fusion(bf16[1,2,60,1152]{3,1,2,0:T(2,128)(2,1)S(1)} %copy-done.1, f32[2,60]{0,1:T(8,128)S(1)} %copy.56, f32[2,60]{0,1:T(8,128)S(1)} %broadcast_multiply_fusion.3, f32[1152]{0:T(1024)S(1)} %copy-done.3, ...), kind=kLoop, calls=%fused_computation.45 | loop fusion | flops 2347656 | bytes 1131360 | tf_op jit(solution)/shard_map/transpose(jvp())/reduce_sum | solution.py:38
  33.6 0.1 copy.61
  33.7 0.1 copy.62
  33.8 0.8 fusion.42
  34.7 0.4 add_reduce_fusion
  35.1 0.0 copy-start.6
  35.1 0.0 copy-start.7
  35.1 0.0 copy-start.8
  35.1 2.5 %all_gather.7 = bf16[4,60,1152]{2,1,0:T(8,128)(2,1)S(1)} all-gather(bf16[2,60,1152]{2,1,0:T(8,128)(2,1)S(1)} %copy.65), channel_id=1, replica_groups=mesh['seq'=4,'dp'=4,'enc'=2] {'enc'}, dimensions={0}, use_global_device_ids=true | all-gather | bytes 829440 | tf_op jit(solution)/shard_map/all_gather | solution.py:108
  37.7 0.1 reshape.238
  37.8 0.1 copy.82
  37.9 0.1 rsqrt.44
  38.0 0.1 div.65
  38.0 0.1 reshape.240
  38.2 0.0 slice-start
  38.2 4.4 %convolution_add_fusion = f32[240,2152]{1,0:T(8,128)S(1)} fusion(bf16[1152,2152]{0,1:T(8,128)(2,1)} %param.22, f32[2152]{0:T(1024)S(1)} %copy-done.7, f32[240,1152]{1,0:T(8,128)S(1)} %reshape.240, f32[1152]{0:T(1024)S(1)} %copy-done.8, f32[1152]{0:T(1024)S(1)} %copy-done.6, f32[240]{0:T(256)S(1)} %rsqrt.44, f32[240]{0:T(256)S(1)} %div.65), kind=kOutput, calls=%fused_computation.2 | convolution fusion | flops 1191868800 | bytes 8149792 | tf_op jit(solution)/shard_map/dot_general | solution.py:112
  42.6 0.0 slice-start.1
  42.6 4.7 %fusion.45 = (f32[2152]{0:T(1024)S(1)}, bf16[240,2152]{1,0:T(8,128)(2,1)S(1)}) fusion(f32[240,2152]{1,0:T(8,128)S(1)} %convolution_add_fusion, bf16[240,1152]{1,0:T(8,128)(2,1)S(1)} %reshape.238, bf16[2152,1152]{1,0:T(8,128)(2,1)} %param.24), kind=kOutput, calls=%fused_computation.101 | convolution fusion | flops 1200297344 | bytes 8618656 | tf_op jit(solution)/shard_map/dot_general | solution.py:114
  47.4 1.6 %fusion.7 = f32[240,1152]{1,0:T(8,128)S(1)} fusion(bf16[1152,2152]{0,1:T(8,128)(2,1)S(1)} %bitcast.108, bf16[240,2152]{1,0:T(8,128)(2,1)S(1)} %get-tuple-element.31), kind=kOutput, calls=%fused_computation.14 | convolution fusion | flops 1189969920 | bytes 7097088 | tf_op jit(solution)/shard_map/dot_general | solution.py:125
  49.0 0.1 reshape.239
  49.1 0.0 copy-start
  49.1 1.8 %copy.70 = f32[4,60,1152]{2,0,1:T(4,128)} copy(f32[4,60,1152]{2,1,0:T(8,128)S(1)} %reshape.239) | data formatting | bytes 2211840 | tf_op jit(solution)/shard_map/reshape | solution.py:131
  50.9 0.0 all-reduce.3.cloned.1.call-update
  50.9 0.4 convert_reduce_fusion
  51.4 0.6 fusion.21
  52.0 0.1 copy.73
  52.0 0.1 copy.74
  52.2 0.3 dynamic_update_slice.3
  52.6 18.3 %all-reduce.3.cloned.1.call-done = f32[4,60,1152]{2,0,1:T(4,128)} async-done(((f32[4,60,1152]{2,0,1:T(4,128)}), f32[4,60,1152]{2,0,1:T(4,128)}) %all-reduce.3.cloned.1.call-update) | async-done | bytes 1105936 | tf_op jit(solution)/shard_map/psum | solution.py:131
  70.9 2.5 %fusion.32 = (f32[1152]{0:T(1024)S(1)}, f32[2,60]{0,1:T(8,128)S(1)}, f32[1152]{0:T(1024)S(1)}) fusion(f32[2,60]{0,1:T(8,128)S(1)} %copy.74, f32[2,60]{0,1:T(8,128)S(1)} %broadcast_multiply_fusion.1, f32[4,60,1152]{2,0,1:T(4,128)} %all-reduce.3.cloned.1.call-done, s32[]{:T(128)S(6)} %select_n.59, bf16[1,4,60,1152]{3,1,2,0:T(4,128)(2,1)S(1)} %copy-done, ...), kind=kLoop, calls=%fused_computation.53 | loop fusion | flops 1241736 | bytes 844708 | tf_op jit(solution)/shard_map/transpose(jvp())/reduce_sum | solution.py:49
  73.4 0.1 stack.27
  73.5 41.2 %all-reduce = (f32[6,1152]{1,0:T(8,128)S(1)}, f32[4304]{0:T(1024)S(1)}) all-reduce(f32[6,1152]{1,0:T(8,128)S(1)} %stack.27, f32[4304]{0:T(1024)S(1)} %dynamic_update_slice.3), channel_id=1, replica_groups=mesh['seq'=4,'dp'=4,'enc'=2] {'seq','dp','enc'}, use_global_device_ids=true, to_apply=%region_26.27 | all-reduce | flops 11216 | bytes 89728 | tf_op jit(solution)/shard_map/psum | solution.py:143
  114.7 0.6 broadcast_multiply_fusion
  115.3 0.6 broadcast_multiply_fusion.4
  115.9 0.1 copy.75
  116.0 0.1 copy.76
  116.1 2.3 %fusion.41 = (f32[2,60]{0,1:T(8,128)S(1)}, f32[2,60,1152]{2,0,1:T(2,128)S(1)}) fusion(f32[2,60]{0,1:T(8,128)S(1)} %copy.76, f32[2,60]{0,1:T(8,128)S(1)} %broadcast_multiply_fusion.1, bf16[1,4,60,1152]{3,1,2,0:T(4,128)(2,1)S(1)} %copy-done, s32[]{:T(128)S(6)} %select_n.59, f32[2,60]{0,1:T(8,128)S(1)} %copy.74, f32[1152]{0:T(1024)S(1)} %copy-done.6, ...), kind=kLoop, calls=%fused_computation.98 | loop fusion | flops 1105800 | bytes 1388932 | tf_op jit(solution)/shard_map/transpose(jvp())/reduce_sum | solution.py:19
  118.5 1.1 fusion.33
  (38 shorter events, 0.2 us)
Async XLA Ops:
  7.2 5.6 %copy-start.2 = (bf16[1,2,48,1152]{3,2,1,0:T(8,128)(2,1)S(1)}, bf16[1,2,48,1152]{3,2,1,0:T(8,128)(2,1)}, u32[]{:S(2)}) copy-start(bf16[1,2,48,1152]{3,2,1,0:T(8,128)(2,1)} %param.14) | copy-start | bytes 663556
  7.2 63.7 %all-reduce.3.cloned.1.call-start = ((), (), s32[]{:S(2)}) async-start(), calls=%async_computation | async-start | bytes 2211840 | tf_op jit(solution)/shard_map/psum | solution.py:131
  9.9 16.7 %copy-start.1 = (bf16[1,2,60,1152]{3,1,2,0:T(2,128)(2,1)S(1)}, bf16[1,2,60,1152]{3,1,2,0:T(2,128)(2,1)}, u32[]{:S(2)}) copy-start(bf16[1,2,60,1152]{3,1,2,0:T(2,128)(2,1)} %param.19) | copy-start | bytes 829444
  11.5 16.1 %copy-start.3 = (f32[1152]{0:T(1024)S(1)}, f32[1152]{0:T(1024)}, u32[]{:S(2)}) copy-start(f32[1152]{0:T(1024)} %param.25) | copy-start | bytes 13828
  11.5 16.1 %copy-start.4 = (f32[1152]{0:T(1024)S(1)}, f32[1152]{0:T(1024)}, u32[]{:S(2)}) copy-start(f32[1152]{0:T(1024)} %param.26) | copy-start | bytes 13828
  12.7 17.0 %copy-start.5 = (f32[1152]{0:T(1024)S(1)}, f32[1152]{0:T(1024)}, u32[]{:S(2)}) copy-start(f32[1152]{0:T(1024)} %param.27) | copy-start | bytes 13828
  35.1 3.1 %copy-start.6 = (f32[1152]{0:T(1024)S(1)}, f32[1152]{0:T(1024)}, u32[]{:S(2)}) copy-start(f32[1152]{0:T(1024)} %param.20) | copy-start | bytes 13828
  35.1 3.1 %copy-start.7 = (f32[2152]{0:T(1024)S(1)}, f32[2152]{0:T(1024)}, u32[]{:S(2)}) copy-start(f32[2152]{0:T(1024)} %param.23) | copy-start | bytes 25828
  35.1 3.1 %copy-start.8 = (f32[1152]{0:T(1024)S(1)}, f32[1152]{0:T(1024)}, u32[]{:S(2)}) copy-start(f32[1152]{0:T(1024)} %param.21) | copy-start | bytes 13828
  38.2 9.1 %slice-start = ((s8[4958208]{0:T(1024)(128)(4,1)}), s8[4194304]{0:T(1024)(128)(4,1)S(1)}, s32[]{:S(2)}) async-start(s8[4958208]{0:T(1024)(128)(4,1)} %bitcast.107), calls=%async_computation.1 | async-start | bytes 8388608
  42.6 4.7 %slice-start.1 = ((s8[4958208]{0:T(1024)(128)(4,1)}), s8[763904]{0:T(1024)(128)(4,1)S(1)}, s32[]{:S(2)}) async-start(s8[4958208]{0:T(1024)(128)(4,1)} %bitcast.107), calls=%async_computation.2 | async-start | bytes 1527808
  49.1 1.8 %copy-start = (bf16[1,4,60,1152]{3,1,2,0:T(4,128)(2,1)S(1)}, bf16[1,4,60,1152]{3,1,2,0:T(4,128)(2,1)}, u32[]{:S(2)}) copy-start(bf16[1,4,60,1152]{3,1,2,0:T(4,128)(2,1)} %param.18) | copy-start | bytes 1658884
Sparse Core Ops, SparseCore 0:
  51.0 19.8 all-reduce.2
where the time goes:
time: 127 us; the launch traced here: 126 us
  blocking collectives  57.4 us (45%)
  other arithmetic  19 us (15%)
  waiting for transfers between devices  18.3 us (14%)
  between operations  14.4 us (11%)
  matrix products  10.7 us (8%)
  local copies, waits for them, and re-layouts  6.55 us (5%)
    psum x1, blocking collectives, body(): norm_sum, fc1_sum = lax.psum((norm_part, fc1_full), ('seq', 'dp', 'enc'))  41.2 us
    psum x1, waiting for transfers between devices, body(): summed = lax.psum(product.reshape(PATCH_GROUP, CAP_TOK, D), 'enc')  18.3 us
    all_gather x1, blocking collectives, body(): portion = lax.all_gather(own_rows, 'seq', axis=1, tiled=True)  13.7 us
    dot_general x1, matrix products, body(): lax.dot_general(all_res.reshape(-1, D), fc2_weight, (((1,), (1,)), ((), (...  4.7 us
    dot_general x1, matrix products, body(): jnp.dot(normed.reshape(-1, D), fc1_weight, preferred_element_type=jnp.flo...  4.4 us
    reduce_sum x2, other arithmetic, layer_norm(): centred = values - row_mean  3.14 us
    reduce_sum x3, other arithmetic, layer_norm(): jnp.mean(centred * centred, axis=-1, keepdims=True) + EPSILON  2.67 us
    all_gather x1, blocking collectives, body(): all_res = lax.all_gather(res_wire, 'enc', axis=0, tiled=True)  2.54 us
  transfers between devices with their start and end apart: 1, of which 1 were waited for; matrix products, arithmetic and copies ran while one was open for 1% of the time, Pallas kernels for 0%

commit v1 on v0

--- a/solution.py
+++ b/solution.py
@@ -128,7 +128,7 @@
         (((1,), (1,)), ((), ())),
         preferred_element_type=jnp.float32,
     )
-    summed = lax.psum(product.reshape(PATCH_GROUP, CAP_TOK, D), "enc")
+    summed = jnp.sum(lax.all_gather(product.reshape(PATCH_GROUP, CAP_TOK, D), "enc"), axis=0)
     upstream = lax.dynamic_slice_in_dim(summed, core_index * own_patches, own_patches, 0)
     own_input = lax.dynamic_slice_in_dim(input_rows, core_index * own_patches, own_patches, 0)
     input_grad, pre_scale_grad, pre_shift_grad = pre_back(own_input, pre_gain, pre_bias, upstream)

time: 127 us -> 118 us (0.929)
  waiting for transfers between devices: 18.3 us -> 9.54 us
    psum x1 -> x0, waiting for transfers between devices: 18.3 us -> none  [body(): summed = lax.psum(product.reshape(PATCH_GROUP, CAP_TOK, D), 'enc')]
    all_gather x0 -> x1, waiting for transfers between devices: none -> 9.53 us  [body(): lax.all_gather(product.reshape(PATCH_GROUP, CAP_TOK, D), 'enc')]
    reduce_sum x0 -> x1, other arithmetic: none -> 2.42 us  [body(): jnp.sum(lax.all_gather(product.reshape(PATCH_GROUP, CAP_TOK, D), 'enc'),...]
    reshape x2 -> x0, local copies, waits for them, and re-layouts: 1.88 us -> none  [body(): summed = lax.psum(product.reshape(PATCH_GROUP, CAP_TOK, D), 'enc')]
    another operation x0 -> x2, local copies, waits for them, and re-layouts: none -> 1.83 us  [body(): lax.all_gather(product.reshape(PATCH_GROUP, CAP_TOK, D), 'enc')]
where the time goes in v1:
time: 118 us
  blocking collectives  57.6 us (49%)
  other arithmetic  18.9 us (16%)
  between operations  14.4 us (12%)
  matrix products  10.7 us (9%)
  waiting for transfers between devices  9.54 us (8%)
  local copies, waits for them, and re-layouts  6.51 us (6%)
    psum x1, blocking collectives, body(): norm_sum, fc1_sum = lax.psum((norm_part, fc1_full), ('seq', 'dp', 'enc'))  41.4 us
    all_gather x1, blocking collectives, body(): portion = lax.all_gather(own_rows, 'seq', axis=1, tiled=True)  13.7 us
    all_gather x1, waiting for transfers between devices, body(): lax.all_gather(product.reshape(PATCH_GROUP, CAP_TOK, D), 'enc')  9.53 us
    dot_general x1, matrix products, body(): lax.dot_general(all_res.reshape(-1, D), fc2_weight, (((1,), (1,)), ((), (...  4.71 us
    dot_general x1, matrix products, body(): jnp.dot(normed.reshape(-1, D), fc1_weight, preferred_element_type=jnp.flo...  4.4 us
    reduce_sum x3, other arithmetic, layer_norm(): jnp.mean(centred * centred, axis=-1, keepdims=True) + EPSILON  2.67 us
    all_gather x1, blocking collectives, body(): all_res = lax.all_gather(res_wire, 'enc', axis=0, tiled=True)  2.54 us
    reduce_sum x1, other arithmetic, body(): jnp.sum(lax.all_gather(product.reshape(PATCH_GROUP, CAP_TOK, D), 'enc'),...  2.42 us
  transfers between devices with their start and end apart: 1, of which 1 were waited for; matrix products, arithmetic and copies ran while one was open for 1% of the time, Pallas kernels for 0%

profile of v1, /device:TPU:0, one launch (start us, length us, event | category | flops | bytes accessed | tf_op | source)
XLA Modules:
  0.0 117.7 jit_solution(6779867924873145190)
XLA Ops:
  7.2 0.0 all-gather.3.cloned.1.call-start
  7.2 0.9 select_reduce_fusion.2
  8.1 0.2 reduce-window.7
  8.3 0.1 fusion.43
  8.4 0.1 select_reduce_fusion.3
  8.5 1.3 %convert_reduce_fusion.2 = f32[4,60]{0,1:T(8,128)S(1)} fusion(bf16[1,4,60,1152]{3,1,2,0:T(4,128)(2,1)} %param.18), kind=kLoop, calls=%fused_computation.44 | loop fusion | flops 552720 | bytes 553920 | tf_op jit(solution)/shard_map/reduce_sum | solution.py:18
  9.9 1.6 %fusion.6 = f32[4,60]{0,1:T(8,128)S(1)} fusion(bf16[1,4,60,1152]{3,1,2,0:T(4,128)(2,1)} %param.18, f32[4,60]{0,1:T(8,128)S(1)} %broadcast_multiply_fusion.2), kind=kLoop, calls=%fused_computation.12 | loop fusion | flops 1105680 | bytes 554880 | tf_op jit(solution)/shard_map/reduce_sum | solution.py:20
  11.5 0.1 copy.92
  11.6 1.1 copy.70
  12.7 0.0 copy-start.5
  12.7 0.2 copy.56
  12.9 13.7 %all-gather = bf16[1,2,192,1152]{3,1,0,2:T(2,128)(2,1)S(1)} all-gather(bf16[1,2,48,1152]{3,1,0,2:T(2,128)(2,1)S(1)} %copy.56), channel_id=2, replica_groups=mesh['seq'=4,'dp'=4,'enc'=2] {'seq'}, dimensions={2}, use_global_device_ids=true | all-gather | bytes 1105920 | tf_op jit(solution)/shard_map/all_gather | solution.py:99
  26.6 0.3 convert_reduce_fusion.1
  26.9 0.5 fusion.14
  27.4 0.1 copy.59
  27.5 0.1 copy.60
  27.6 0.0 copy-done.3
  27.6 0.0 copy-done.4
  27.6 0.7 multiply_reduce_fusion.1
  28.3 0.1 copy.61
  28.4 0.1 copy.62
  28.6 1.2 gather_fusion
  29.7 1.7 %fusion.27 = (f32[1152]{0:T(1024)S(1)}, f32[2,60]{0,1:T(8,128)S(1)}, bf16[60,2,1152]{2,1,0:T(2,128)(2,1)S(1)}) fusion(f32[2,60]{0,1:T(8,128)S(1)} %copy.62, f32[1152]{0:T(1024)S(1)} %copy-done.4, f32[1152]{0:T(1024)S(1)} %copy-done.3, f32[2,60]{0,1:T(8,128)S(1)} %copy.60, f32[2,60]{0,1:T(8,128)S(1)} %broadcast_multiply_fusion.3, ...), kind=kLoop, calls=%fused_computation.43 | loop fusion | flops 1934088 | bytes 849912 | tf_op jit(solution)/shard_map/transpose(jvp())/reduce_sum | solution.py:38
  31.5 0.1 copy.63
  31.6 0.1 copy.64
  31.7 1.9 %multiply_reduce_fusion = (f32[1152]{0:T(1024)S(1)}, f32[2,60]{0,1:T(8,128)S(1)}, f32[1152]{0:T(1024)S(1)}, f32[2,60,1152]{2,0,1:T(2,128)S(1)}) fusion(bf16[1,2,60,1152]{3,1,2,0:T(2,128)(2,1)S(1)} %copy-done.1, f32[2,60]{0,1:T(8,128)S(1)} %copy.60, f32[2,60]{0,1:T(8,128)S(1)} %broadcast_multiply_fusion.3, f32[1152]{0:T(1024)S(1)} %copy-done.3, ...), kind=kLoop, calls=%fused_computation.45 | loop fusion | flops 2347656 | bytes 1131360 | tf_op jit(solution)/shard_map/transpose(jvp())/reduce_sum | solution.py:38
  33.6 0.1 copy.65
  33.7 0.1 copy.66
  33.8 0.8 fusion.42
  34.6 0.4 add_reduce_fusion
  35.1 0.0 copy-start.6
  35.1 0.0 copy-start.7
  35.1 0.0 copy-start.8
  35.1 2.5 %all_gather.10 = bf16[4,60,1152]{2,1,0:T(8,128)(2,1)S(1)} all-gather(bf16[2,60,1152]{2,1,0:T(8,128)(2,1)S(1)} %copy.69), channel_id=1, replica_groups=mesh['seq'=4,'dp'=4,'enc'=2] {'enc'}, dimensions={0}, use_global_device_ids=true | all-gather | bytes 829440 | tf_op jit(solution)/shard_map/all_gather | solution.py:108
  37.6 0.1 reshape.235
  37.8 0.1 copy.93
  37.9 0.1 rsqrt.44
  37.9 0.1 div.65
  38.0 0.1 reshape.236
  38.2 0.0 slice-start
  38.2 4.4 %convolution_add_fusion = f32[240,2152]{1,0:T(8,128)S(1)} fusion(bf16[1152,2152]{0,1:T(8,128)(2,1)} %param.22, f32[2152]{0:T(1024)S(1)} %copy-done.7, f32[240,1152]{1,0:T(8,128)S(1)} %reshape.236, f32[1152]{0:T(1024)S(1)} %copy-done.8, f32[1152]{0:T(1024)S(1)} %copy-done.6, f32[240]{0:T(256)S(1)} %rsqrt.44, f32[240]{0:T(256)S(1)} %div.65), kind=kOutput, calls=%fused_computation.2 | convolution fusion | flops 1191868800 | bytes 8149792 | tf_op jit(solution)/shard_map/dot_general | solution.py:112
  42.6 0.0 slice-start.1
  42.6 4.7 %fusion.45 = (f32[2152]{0:T(1024)S(1)}, bf16[240,2152]{1,0:T(8,128)(2,1)S(1)}) fusion(f32[240,2152]{1,0:T(8,128)S(1)} %convolution_add_fusion, bf16[240,1152]{1,0:T(8,128)(2,1)S(1)} %reshape.235, bf16[2152,1152]{1,0:T(8,128)(2,1)} %param.24), kind=kOutput, calls=%fused_computation.101 | convolution fusion | flops 1200297344 | bytes 8618656 | tf_op jit(solution)/shard_map/dot_general | solution.py:114
  47.4 1.6 %fusion.7 = f32[240,1152]{1,0:T(8,128)S(1)} fusion(bf16[1152,2152]{0,1:T(8,128)(2,1)S(1)} %bitcast.108, bf16[240,2152]{1,0:T(8,128)(2,1)S(1)} %get-tuple-element.31), kind=kOutput, calls=%fused_computation.14 | convolution fusion | flops 1189969920 | bytes 7097088 | tf_op jit(solution)/shard_map/dot_general | solution.py:125
  49.0 0.1 all_gather_reshape.3
  49.1 0.0 copy-start
  49.1 1.7 %copy.74 = f32[1,4,60,1152]{3,1,2,0:T(4,128)} copy(f32[1,4,60,1152]{3,2,1,0:T(8,128)S(1)} %all_gather_reshape.3) | data formatting | bytes 2211840 | tf_op jit(solution)/shard_map/all_gather;reshape | solution.py:131
  50.8 0.0 all-gather.3.cloned.1.call-update
  50.9 0.4 convert_reduce_fusion
  51.3 0.6 fusion.21
  51.9 0.1 copy.79
  52.0 0.1 copy.80
  52.2 0.3 dynamic_update_slice.3
  52.5 9.5 %all-gather.3.cloned.1.call-done = f32[2,4,60,1152]{3,1,2,0:T(4,128)} async-done(((f32[1,4,60,1152]{3,1,2,0:T(4,128)}), f32[2,4,60,1152]{3,1,2,0:T(4,128)}) %all-gather.3.cloned.1.call-update) | async-done | bytes 2211856 | tf_op jit(solution)/shard_map/all_gather | solution.py:131
  62.0 2.4 %reduce_sum.284 = f32[4,60,1152]{2,0,1:T(4,128)S(1)} reduce(f32[2,4,60,1152]{3,1,2,0:T(4,128)} %all-gather.3.cloned.1.call-done, f32[]{:T(128)} %constant.33.clone.1), dimensions={0}, to_apply=%region_15.16 | reduce | flops 276480 | bytes 3317764 | tf_op jit(solution)/shard_map/reduce_sum | solution.py:131
  64.5 1.3 %fusion.32 = (f32[1152]{0:T(1024)S(1)}, f32[2,60]{0,1:T(8,128)S(1)}, f32[1152]{0:T(1024)S(1)}) fusion(f32[2,60]{0,1:T(8,128)S(1)} %copy.80, f32[2,60]{0,1:T(8,128)S(1)} %broadcast_multiply_fusion.1, f32[4,60,1152]{2,0,1:T(4,128)S(1)} %reduce_sum.284, s32[]{:T(128)S(6)} %select_n.59, bf16[1,4,60,1152]{3,1,2,0:T(4,128)(2,1)S(1)} %copy-done, f32[1152]{0:T(1024)S(1)} %copy-done.6), kind=kLoop, calls=%fused_computation.53 | loop fusion | flops 1241736 | bytes 844708 | tf_op jit(solution)/shard_map/transpose(jvp())/reduce_sum | solution.py:49
  65.8 0.1 stack.27
  65.8 41.4 %all-reduce = (f32[6,1152]{1,0:T(8,128)S(1)}, f32[4304]{0:T(1024)S(1)}) all-reduce(f32[6,1152]{1,0:T(8,128)S(1)} %stack.27, f32[4304]{0:T(1024)S(1)} %dynamic_update_slice.3), channel_id=1, replica_groups=mesh['seq'=4,'dp'=4,'enc'=2] {'seq','dp','enc'}, use_global_device_ids=true, to_apply=%region_26.27 | all-reduce | flops 11216 | bytes 89728 | tf_op jit(solution)/shard_map/psum | solution.py:143
  107.2 0.6 broadcast_multiply_fusion
  107.9 0.6 broadcast_multiply_fusion.4
  108.5 0.1 copy.81
  108.6 0.1 copy.82
  108.7 1.1 fusion.41
  109.8 1.1 fusion.33
  (39 shorter events, 0.2 us)
Async XLA Ops:
  7.2 5.6 %copy-start.2 = (bf16[1,2,48,1152]{3,2,1,0:T(8,128)(2,1)S(1)}, bf16[1,2,48,1152]{3,2,1,0:T(8,128)(2,1)}, u32[]{:S(2)}) copy-start(bf16[1,2,48,1152]{3,2,1,0:T(8,128)(2,1)} %param.14) | copy-start | bytes 663556
  7.2 54.9 %all-gather.3.cloned.1.call-start = ((), (), s32[]{:S(2)}) async-start(), calls=%async_computation | async-start | bytes 3317760 | tf_op jit(solution)/shard_map/all_gather | solution.py:131
  9.9 16.7 %copy-start.1 = (bf16[1,2,60,1152]{3,1,2,0:T(2,128)(2,1)S(1)}, bf16[1,2,60,1152]{3,1,2,0:T(2,128)(2,1)}, u32[]{:S(2)}) copy-start(bf16[1,2,60,1152]{3,1,2,0:T(2,128)(2,1)} %param.19) | copy-start | bytes 829444
  11.5 16.1 %copy-start.3 = (f32[1152]{0:T(1024)S(1)}, f32[1152]{0:T(1024)}, u32[]{:S(2)}) copy-start(f32[1152]{0:T(1024)} %param.25) | copy-start | bytes 13828
  11.5 16.1 %copy-start.4 = (f32[1152]{0:T(1024)S(1)}, f32[1152]{0:T(1024)}, u32[]{:S(2)}) copy-start(f32[1152]{0:T(1024)} %param.26) | copy-start | bytes 13828
  12.7 17.0 %copy-start.5 = (f32[1152]{0:T(1024)S(1)}, f32[1152]{0:T(1024)}, u32[]{:S(2)}) copy-start(f32[1152]{0:T(1024)} %param.27) | copy-start | bytes 13828
  35.1 3.1 %copy-start.6 = (f32[1152]{0:T(1024)S(1)}, f32[1152]{0:T(1024)}, u32[]{:S(2)}) copy-start(f32[1152]{0:T(1024)} %param.20) | copy-start | bytes 13828
  35.1 3.1 %copy-start.7 = (f32[2152]{0:T(1024)S(1)}, f32[2152]{0:T(1024)}, u32[]{:S(2)}) copy-start(f32[2152]{0:T(1024)} %param.23) | copy-start | bytes 25828
  35.1 3.1 %copy-start.8 = (f32[1152]{0:T(1024)S(1)}, f32[1152]{0:T(1024)}, u32[]{:S(2)}) copy-start(f32[1152]{0:T(1024)} %param.21) | copy-start | bytes 13828
  38.2 9.2 %slice-start = ((s8[4958208]{0:T(1024)(128)(4,1)}), s8[4194304]{0:T(1024)(128)(4,1)S(1)}, s32[]{:S(2)}) async-start(s8[4958208]{0:T(1024)(128)(4,1)} %bitcast.107), calls=%async_computation.1 | async-start | bytes 8388608
  42.6 4.7 %slice-start.1 = ((s8[4958208]{0:T(1024)(128)(4,1)}), s8[763904]{0:T(1024)(128)(4,1)S(1)}, s32[]{:S(2)}) async-start(s8[4958208]{0:T(1024)(128)(4,1)} %bitcast.107), calls=%async_computation.2 | async-start | bytes 1527808
  49.1 1.8 %copy-start = (bf16[1,4,60,1152]{3,1,2,0:T(4,128)(2,1)S(1)}, bf16[1,4,60,1152]{3,1,2,0:T(4,128)(2,1)}, u32[]{:S(2)}) copy-start(bf16[1,4,60,1152]{3,1,2,0:T(4,128)(2,1)} %param.18) | copy-start | bytes 1658884
Sparse Core Ops, SparseCore 0:
  51.0 11.0 all-gather.2
